TPU v7x, 256 devices: a whole 4x4x8 slice. The times are simulated.
256 devices in a mesh: shot: 64 (over x, y_lo, z), freq: 4 (over y_hi, core).
Axes of the slice: x: 4, y: 4 (y_hi: 2, y_lo: 2; y = y_hi * 2 + y_lo), z: 8, core: 2. Of those that a mesh axis runs over, the one named last changes fastest.
Arguments:
- data: bfloat16 [4, 2, 8192, 8192], P('freq', None, 'shot'), may hold values from -6 to 6
- primaries: bfloat16 [4, 2, 8192, 640], P('freq', None, 'shot'), may hold values from -0.15625 to 0.15625
- wavelet: float32 [4, 2], P('freq'), may hold values from 2 to 8
- cover_ids: int32 [8192, 8], P('shot'), may hold values from 0 to 15, all different within a row
- cover_counts: int32 [8192], P('shot'), may hold values from 1 to 8
Outputs:
- misfit: bfloat16 [4, 2, 8192, 8192], P('freq', None, 'shot')
- grad_primaries: float32 [4, 2, 8192, 640], P('freq', None, 'shot')
- wavelet_grad: float32 [128], replicated
Inputs may be any that keep to these rules, and one draw needn't show every extreme that they name: `cover_ids`: the entries of a shot's list are different coverage blocks.
All inputs are finite; a program needn't handle non-finite values.
Results may differ from a plain program's by a relative error of at most 0.0013.
Values may be sent and summed in bfloat16 or wider, within the bound.
A program may use at most 128 MiB of HBM per device.

v0:
```python
import math

import jax
import jax.numpy as jnp
from jax import lax
from jax.sharding import PartitionSpec as P

RB = 512
NT = 128


def passed_along(block, axis, distance):
    devices = range(lax.axis_size(axis))
    route = [(i - distance, i) for i in devices if i - distance in devices]
    return lax.ppermute(block, axis, route)


def on_device(data, primaries, wavelet, cover_ids, cover_counts):
    own_rows = data[0]
    rows_dev = own_rows.shape[1]
    width = own_rows.shape[2]
    band_width = primaries.shape[3]
    reach_blocks = (band_width // rows_dev - 1) // 2
    shot_count = lax.axis_size("shot") * rows_dev
    stride_cols = width // shot_count
    position = lax.axis_index("shot")
    freq_index = lax.axis_index("freq")
    lower_rows = [
        passed_along(own_rows, "shot", distance) for distance in range(reach_blocks, 0, -1)
    ]
    upper_rows = [
        passed_along(own_rows, "shot", -distance) for distance in range(1, reach_blocks + 1)
    ]
    nearby = jnp.concatenate(lower_rows + [own_rows] + upper_rows, axis=1)
    first_row = (position - reach_blocks) * rows_dev
    shot_ids = first_row + jnp.arange(band_width, dtype=jnp.int32)
    columns = jnp.arange(width, dtype=jnp.int32)
    direct_hit = columns[None, :] == shot_ids[:, None] * stride_cols
    wave_re = wavelet[0, 0]
    wave_im = wavelet[0, 1]
    operand = jnp.stack(
        [
            jnp.where(direct_hit, wave_re, 0.0) - nearby[0].astype(jnp.float32),
            jnp.where(direct_hit, wave_im, 0.0) - nearby[1].astype(jnp.float32),
        ]
    ).astype(jnp.bfloat16)
    response = primaries[0]
    response_pair = jnp.stack(
        [jnp.stack([response[0], -response[1]]), jnp.stack([response[1], response[0]])]
    )
    predicted = jnp.einsum(
        "gcik,ckj->gij", response_pair, operand, preferred_element_type=jnp.float32
    )
    block_ids = jnp.arange(width // RB, dtype=jnp.int32)
    listed = jnp.arange(cover_ids.shape[1], dtype=jnp.int32)[None, :] < cover_counts[:, None]
    covered = jnp.any(
        (cover_ids[:, :, None] == block_ids[None, None, :]) & listed[:, :, None], axis=1
    )
    receiver_mask = jnp.repeat(covered.astype(jnp.float32), RB, axis=1)
    misfit = (receiver_mask[None] * (own_rows.astype(jnp.float32) - predicted)).astype(jnp.bfloat16)
    misfit_pair = jnp.stack([misfit, jnp.stack([misfit[1], -misfit[0]])])
    gradient = -jnp.einsum(
        "gcij,ckj->gik", misfit_pair, operand, preferred_element_type=jnp.float32
    )
    sources = jnp.pad(misfit, ((0, 0), (0, 0), (reach_blocks * rows_dev, reach_blocks * rows_dev)))
    sources = lax.dynamic_slice_in_dim(sources, position * rows_dev, band_width, 2).astype(
        jnp.float32
    )
    response_wide = response.astype(jnp.float32)
    corr_re = -jnp.sum(response_wide[0] * sources[0] + response_wide[1] * sources[1])
    corr_im = -jnp.sum(response_wide[0] * sources[1] - response_wide[1] * sources[0])
    times = jnp.arange(NT, dtype=jnp.int32).astype(jnp.float32)
    phase = 2.0 * math.pi * (freq_index + 1).astype(jnp.float32) * times / NT
    scale = 1.0 / math.sqrt(shot_count * band_width)
    total_re, total_im = lax.psum((corr_re, corr_im), "shot")
    series = total_re * jnp.cos(phase) - total_im * jnp.sin(phase)
    wavelet_grad = lax.psum(series, "freq") * scale
    return (misfit[None], gradient[None], wavelet_grad)


def solution(mesh):
    in_specs = (
        P("freq", None, "shot", None),
        P("freq", None, "shot", None),
        P("freq", None),
        P("shot", None),
        P("shot"),
    )
    out_specs = (P("freq", None, "shot", None), P("freq", None, "shot", None), P())
    return jax.shard_map(
        on_device, mesh=mesh, in_specs=in_specs, out_specs=out_specs, check_vma=False
    )
```

profile of v0, /device:TPU:1, one launch (start us, length us, event | category | flops | bytes accessed | tf_op | source)
XLA Modules:
  0.0 498.0 jit_solution(17625872059243874326)
XLA Ops:
  0.6 7.7 %collective-permute-start = (bf16[2,128,8192]{2,1,0:T(8,128)(2,1)}, bf16[2,128,8192]{2,1,0:T(8,128)(2,1)}, u32[]{:S(2)}, u32[]{:S(2)}) collective-permute-start(bf16[2,128,8192]{2,1,0:T(8,128)(2,1)} %bitcast.71), channel_id=1, source_target_pairs={{0,8},{4,12},{8,16},{12,20},{16,24},{20,28},{24,32},{28,36},{32,40... | collective-permute-start | bytes 12582920 | tf_op jit(solution)/shard_map/ppermute | solution.py:15
  8.3 5.5 %collective-permute-start.1 = (bf16[2,128,8192]{2,1,0:T(8,128)(2,1)}, bf16[2,128,8192]{2,1,0:T(8,128)(2,1)}, u32[]{:S(2)}, u32[]{:S(2)}) collective-permute-start(bf16[2,128,8192]{2,1,0:T(8,128)(2,1)} %bitcast.72), channel_id=1, source_target_pairs={{0,4},{4,8},{8,12},{12,16},{16,20},{20,24},{24,28},{28,32},{32,36}... | collective-permute-start | bytes 12582920 | tf_op jit(solution)/shard_map/ppermute | solution.py:15
  13.8 1.3 collective-permute-start.2
  15.1 1.3 collective-permute-start.3
  16.4 1.4 fusion.28
  17.8 0.7 iota_compare_fusion.2
  18.4 0.7 fusion.23
  19.1 0.9 fusion.26
  20.1 1.0 slice_bitcast_fusion.2
  21.1 1.0 convert_element_type.38
  22.2 0.1 copy.9
  22.3 0.3 broadcast_in_dim.28
  22.6 5.4 %copy.12 = f32[16,8,16,512]{3,1,2,0:T(8,128)} copy(f32[16,8,16,512]{3,2,1,0:T(8,128)S(1)} %bitcast.70) | data formatting | bytes 8388608
  28.0 0.0 copy-start.1
  28.0 0.9 maximum_bitcast_fusion.18
  28.9 102.8 %collective-permute-done = bf16[2,128,8192]{2,1,0:T(8,128)(2,1)} collective-permute-done((bf16[2,128,8192]{2,1,0:T(8,128)(2,1)}, bf16[2,128,8192]{2,1,0:T(8,128)(2,1)}, u32[]{:S(2)}, u32[]{:S(2)}) %collective-permute-start) | collective-permute-done | bytes 4194336 | tf_op jit(solution)/shard_map/ppermute | solution.py:15
  131.7 2.5 constant_dynamic-update-slice_fusion.4
  134.2 141.6 %collective-permute-done.1 = bf16[2,128,8192]{2,1,0:T(8,128)(2,1)} collective-permute-done((bf16[2,128,8192]{2,1,0:T(8,128)(2,1)}, bf16[2,128,8192]{2,1,0:T(8,128)(2,1)}, u32[]{:S(2)}, u32[]{:S(2)}) %collective-permute-start.1) | collective-permute-done | bytes 4194336 | tf_op jit(solution)/shard_map/ppermute | solution.py:15
  275.8 2.5 constant_dynamic-update-slice_fusion.3
  278.2 0.0 copy-done.1
  278.2 0.4 constant_dynamic-update-slice_fusion.2
  278.7 0.0 collective-permute-done.2
  278.7 2.5 constant_dynamic-update-slice_fusion.1
  281.1 4.2 collective-permute-done.3
  285.3 2.5 constant_dynamic-update-slice_fusion
  287.8 11.5 %subtract_convert_fusion.1 = (bf16[1,640,8192]{2,1,0:T(8,128)(2,1)}, bf16[1,640,8192]{2,1,0:T(8,128)(2,1)}) fusion(bf16[2,640,8192]{2,1,0:T(8,128)(2,1)S(1)} %constant_dynamic-update-slice_fusion, f32[]{:T(128)} %bitcast.5, s32[640]{0:T(1024)S(1)} %iota_add_fusion, f32[]{:T(128)} %bitcast.6), kind=kLoop, calls=%fused_computation.2 | loop fusion | flops 47185920 | bytes 41945608 | tf_op jit(solution)/shard_map/convert
  299.2 12.9 %fusion.5 = bf16[2,128,8192]{2,1,0:T(8,128)(2,1)S(1)} fusion(bf16[1,640,8192]{2,1,0:T(8,128)(2,1)} %get-tuple-element.8, bf16[1,640,8192]{2,1,0:T(8,128)(2,1)} %get-tuple-element.7, f32[128,8192]{1,0:T(8,128)} %bitcast.75, bf16[1,2,128,640]{3,2,1,0:T(8,128)(2,1)} %get-tuple-element.14, bf16[1,2,128,640]{3,2,1,0:T(8,128)(2,1)} %get-tuple-element.13, ...), kind=kOutput, calls=%fused_computation.9 | convolution fusion | flops 5387911168 | bytes 34209792 | tf_op jit(solution)/shard_map/gcik,ckj->gij/dot_general | solution.py:51
  312.1 0.0 copy-start
  312.1 2.0 copy-done
  314.1 0.1 fusion.21
  314.2 0.7 add_reduce_fusion
  316.2 3.8 fusion.27
  320.1 125.5 %all-reduce.1 = (f32[]{:T(128)}, f32[]{:T(128)}) all-reduce(f32[]{:T(128)S(6)} %neg.27, f32[]{:T(128)S(6)} %neg.26), channel_id=1, replica_groups=mesh['shot'=64,'freq'=4] {'shot'}, use_global_device_ids=true, to_apply=%region_4.5 | all-reduce | flops 2 | bytes 16 | tf_op jit(solution)/shard_map/psum | solution.py:75
  445.6 1.3 multiply_subtract_fusion
  446.9 36.1 %psum.23 = f32[128]{0:T(128)S(1)} all-reduce(f32[128]{0:T(128)S(1)} %multiply_subtract_fusion), channel_id=1, replica_groups=mesh['shot'=64,'freq'=4] {'freq'}, use_global_device_ids=true, to_apply=%region_5.6 | all-reduce | flops 128 | bytes 1024 | tf_op jit(solution)/shard_map/psum | solution.py:77
  483.0 0.5 broadcast_multiply_fusion
  483.5 2.0 maximum_bitcast_fusion.11
  485.5 12.5 %fusion.15 = f32[1,2,128,640]{3,2,1,0:T(8,128)} fusion(bf16[1,640,8192]{2,1,0:T(8,128)(2,1)} %get-tuple-element.8, bf16[1,640,8192]{2,1,0:T(8,128)(2,1)} %get-tuple-element.7, bf16[1,2,128,8192]{3,2,1,0:T(8,128)(2,1)S(1)} %maximum_bitcast_fusion.11, bf16[1,2,128,8192]{3,2,1,0:T(8,128)(2,1)} %bitcast.68), kind=kOutput, calls=%fused_computation.18 | convolution fusion | flops 5383553024 | bytes 30015488 | tf_op jit(solution)/shard_map/gcij,ckj->gik/dot_general | solution.py:62
  (2 shorter events, 0.0 us)
Async XLA Ops:
  0.6 131.1 %collective-permute-start = (bf16[2,128,8192]{2,1,0:T(8,128)(2,1)}, bf16[2,128,8192]{2,1,0:T(8,128)(2,1)}, u32[]{:S(2)}, u32[]{:S(2)}) collective-permute-start(bf16[2,128,8192]{2,1,0:T(8,128)(2,1)} %bitcast.71), channel_id=1, source_target_pairs={{0,8},{4,12},{8,16},{12,20},{16,24},{20,28},{24,32},{28,36},{32,40... | collective-permute-start | bytes 12582920 | tf_op jit(solution)/shard_map/ppermute | solution.py:15
  8.3 267.5 %collective-permute-start.1 = (bf16[2,128,8192]{2,1,0:T(8,128)(2,1)}, bf16[2,128,8192]{2,1,0:T(8,128)(2,1)}, u32[]{:S(2)}, u32[]{:S(2)}) collective-permute-start(bf16[2,128,8192]{2,1,0:T(8,128)(2,1)} %bitcast.72), channel_id=1, source_target_pairs={{0,4},{4,8},{8,12},{12,16},{16,20},{20,24},{24,28},{28,32},{32,36}... | collective-permute-start | bytes 12582920 | tf_op jit(solution)/shard_map/ppermute | solution.py:15
  13.8 264.9 %collective-permute-start.2 = (bf16[2,128,8192]{2,1,0:T(8,128)(2,1)}, bf16[2,128,8192]{2,1,0:T(8,128)(2,1)}, u32[]{:S(2)}, u32[]{:S(2)}) collective-permute-start(bf16[2,128,8192]{2,1,0:T(8,128)(2,1)} %bitcast.73), channel_id=1, source_target_pairs={{4,0},{8,4},{12,8},{16,12},{20,16},{24,20},{28,24},{32,28},{36,32}... | collective-permute-start | bytes 12582920 | tf_op jit(solution)/shard_map/ppermute | solution.py:15
  15.1 270.2 %collective-permute-start.3 = (bf16[2,128,8192]{2,1,0:T(8,128)(2,1)}, bf16[2,128,8192]{2,1,0:T(8,128)(2,1)}, u32[]{:S(2)}, u32[]{:S(2)}) collective-permute-start(bf16[2,128,8192]{2,1,0:T(8,128)(2,1)} %bitcast.74), channel_id=1, source_target_pairs={{8,0},{12,4},{16,8},{20,12},{24,16},{28,20},{32,24},{36,28},{40,32... | collective-permute-start | bytes 12582920 | tf_op jit(solution)/shard_map/ppermute | solution.py:15
  28.0 250.2 %copy-start.1 = (bf16[1,2,128,8192]{3,2,1,0:T(8,128)(2,1)S(1)}, bf16[1,2,128,8192]{3,2,1,0:T(8,128)(2,1)}, u32[]{:S(2)}) copy-start(bf16[1,2,128,8192]{3,2,1,0:T(8,128)(2,1)} %param.5) | copy-start | bytes 12582916
  312.1 2.0 copy-start
where the time goes:
time: 499 us; the launch traced here: 498 us
  waiting for transfers between devices  249 us (50%)
  blocking collectives  162 us (32%)
  matrix products  25.4 us (5%)
  other arithmetic  24.1 us (5%)
  local copies, waits for them, and re-layouts  20.5 us (4%)
  starting transfers between devices  15.7 us (3%)
    ppermute x4, waiting for transfers between devices, passed_along(): return lax.ppermute(block, axis, route)  249 us
    psum x1, blocking collectives, on_device(): total_re, total_im = lax.psum((corr_re, corr_im), 'shot')  126 us
    psum x1, blocking collectives, on_device(): wavelet_grad = lax.psum(series, 'freq') * scale  36.1 us
    ppermute x4, starting transfers between devices, passed_along(): return lax.ppermute(block, axis, route)  15.7 us
    unnamed x9, local copies, waits for them, and re-layouts  15.2 us
    dot_general x1, matrix products, on_device(): jnp.einsum('gcik,ckj->gij', response_pair, operand, preferred_element_typ...  12.9 us
    dot_general x1, matrix products, on_device(): jnp.einsum('gcij,ckj->gik', misfit_pair, operand, preferred_element_type=...  12.5 us
    another operation x1, other arithmetic  11.5 us
  transfers between devices with their start and end apart: 4, of which 3 were waited for; matrix products, arithmetic and copies ran while one was open for 4% of the time, Pallas kernels for 0%

commit v1 on v0

v1 whole, which is shorter than its diff:
```python
import functools
import math

import jax
import jax.numpy as jnp
import numpy as np
from jax import lax
from jax.experimental import pallas as pl
from jax.experimental.pallas import tpu as pltpu
from jax.sharding import PartitionSpec as P

RB = 512
NT = 128
REACH = 2
PRE = 3
LAG = 4
RADIX = 4
MESH = pl.DeviceIdType.MESH


def kernel(
    dims,
    data,
    prim,
    wave,
    ids,
    counts,
    waves,
    misfit,
    grad,
    wavelet_grad,
    rec,
    own,
    near,
    mix,
    outer,
    stage,
    window,
    sums,
    own_sem,
    rec_sem,
    out_sem,
    send_sem,
    recv_sem,
    sum_send_sem,
    sum_recv_sem,
):
    shots, freqs, chunks, rows = dims
    width = own.shape[3]
    tiles = width // rows
    me = lax.axis_index("shot")
    freq = lax.axis_index("freq")
    right = lax.rem(me + 1, shots)
    left = lax.rem(me + shots - 1, shots)

    def first_of(block):
        return lax.rem(lax.div(block, tiles) + chunks - 1, chunks)

    own_first = first_of(me)
    left_first = first_of(left)
    right_first = first_of(right)
    work_first = lax.rem(lax.div(me + shots - REACH, tiles), chunks)

    def load_own(chunk):
        columns = pl.ds(pl.multiple_of(chunk * width, width), width)
        return pltpu.make_async_copy(
            data.at[0, :, :, columns], own.at[chunk], own_sem.at[chunk]
        )

    load_rec = pltpu.make_async_copy(data.at[0], rec, rec_sem.at[0])

    def hop(stream, chunk):
        src = own.at[chunk] if stream < 2 else near.at[stream - 2, chunk]
        target = right if stream % 2 == 0 else left
        return pltpu.make_async_remote_copy(
            src_ref=src,
            dst_ref=near.at[stream, chunk],
            send_sem=send_sem.at[stream, chunk],
            recv_sem=recv_sem.at[stream, chunk],
            device_id=(target, freq),
            device_id_type=MESH,
        )

    digits = [freq, lax.rem(me, 4), lax.rem(lax.div(me, 4), 4), lax.div(me, 16)]

    def partner(level, digit):
        if level == 0:
            return (me, digit)
        scale = (1, 4, 16)[level - 1]
        return (me + (digit - digits[level]) * scale, freq)

    def exchange(level, step):
        digit = lax.rem(digits[level] + step, RADIX)
        return pltpu.make_async_remote_copy(
            src_ref=sums.at[level, digits[level]],
            dst_ref=sums.at[level, digits[level]],
            send_sem=sum_send_sem.at[level, step - 1],
            recv_sem=sum_recv_sem.at[level, digits[level]],
            device_id=partner(level, digit),
            device_id_type=MESH,
        )

    def arrival(level, step):
        digit = lax.rem(digits[level] + step, RADIX)
        return pltpu.make_async_remote_copy(
            src_ref=sums.at[level, digit],
            dst_ref=sums.at[level, digit],
            send_sem=sum_send_sem.at[level, step - 1],
            recv_sem=sum_recv_sem.at[level, digit],
            device_id=partner(level, digit),
            device_id_type=MESH,
        )

    def sum_send(level, value):
        sums[level, digits[level]] = value
        for step in range(1, RADIX):
            exchange(level, step).start()

    def sum_take(level):
        for step in range(1, RADIX):
            arrival(level, step).wait_recv()
        total = sums[level, 0]
        for digit in range(1, RADIX):
            total = total + sums[level, digit]
        return total

    for step in range(chunks):
        load_own(lax.rem(own_first + step, chunks)).start()
    load_rec.start()

    barrier = pltpu.get_barrier_semaphore()
    for target in (left, right):
        pl.semaphore_signal(barrier, inc=1, device_id=(target, freq), device_id_type=MESH)
    for level in range(4):
        for step in range(1, RADIX):
            pl.semaphore_signal(
                barrier,
                inc=1,
                device_id=partner(level, lax.rem(digits[level] + step, RADIX)),
                device_id_type=MESH,
            )
    pl.semaphore_wait(barrier, 2 + 4 * (RADIX - 1))

    diagonal = lax.broadcasted_iota(jnp.int32, (rows, rows), 0) == lax.broadcasted_iota(
        jnp.int32, (rows, rows), 1
    )
    for step in range(PRE):
        chunk = lax.rem(own_first + step, chunks)
        load_own(chunk).wait()
        if step == 1:
            spot = pl.ds(pl.multiple_of(lax.rem(me, tiles) * rows, rows), rows)
            for part in range(2):
                tile = own[chunk, part, :, spot]
                moved = (tile.astype(jnp.float32) - wave[0, part]).astype(jnp.bfloat16)
                own[chunk, part, :, spot] = jnp.where(diagonal, moved, tile)
        for stream in range(2):
            hop(stream, chunk).start()

    def inside(block):
        there = me + block - REACH
        return jnp.where(jnp.logical_and(there >= 0, there < shots), 1.0, 0.0)

    def response(part, block):
        tile = prim[0, part, :, pl.ds(block * rows, rows)]
        return tile.astype(jnp.float32) * inside(block)

    for block in range(2 * REACH + 1):
        real = response(0, block)
        imag = response(1, block)
        mix[block, pl.ds(0, rows), pl.ds(0, rows)] = real.astype(jnp.bfloat16)
        mix[block, pl.ds(0, rows), pl.ds(rows, rows)] = (-imag).astype(jnp.bfloat16)
        mix[block, pl.ds(rows, rows), pl.ds(0, rows)] = imag.astype(jnp.bfloat16)
        mix[block, pl.ds(rows, rows), pl.ds(rows, rows)] = real.astype(jnp.bfloat16)
    outer[...] = jnp.zeros_like(outer)
    load_rec.wait()

    def rows_of(block, chunk):
        ref = own.at[chunk] if block == REACH else near.at[(2, 0, -1, 1, 3)[block], chunk]
        return ref[...].reshape(2 * rows, width)

    def out_copy(slot, chunk):
        columns = pl.ds(pl.multiple_of(chunk * width, width), width)
        return pltpu.make_async_copy(
            stage.at[slot], misfit.at[0, :, :, columns], out_sem.at[slot]
        )

    def work(step):
        chunk = lax.rem(work_first + step, chunks)
        slot = lax.rem(step, 2)
        for stream in (2, 3):
            hop(stream, chunk).wait_recv()
        columns = pl.ds(pl.multiple_of(chunk * width, width), width)
        predicted = jnp.dot(mix[0], rows_of(0, chunk), preferred_element_type=jnp.float32)
        for block in range(1, 2 * REACH + 1):
            predicted += jnp.dot(
                mix[block], rows_of(block, chunk), preferred_element_type=jnp.float32
            )
        entry = lax.broadcasted_iota(jnp.int32, ids.shape, 1)
        hit = jnp.logical_and(ids[...] == chunk, entry < counts[...])
        mask = jnp.sum(jnp.where(hit, 1.0, 0.0), axis=1, keepdims=True)
        record = rec[:, :, columns].astype(jnp.float32)
        residual = (mask[None] * (record + predicted.reshape(2, rows, width))).astype(
            jnp.bfloat16
        )

        @pl.when(step >= 2)
        def _():
            out_copy(slot, chunk).wait()

        stage[slot] = residual
        out_copy(slot, chunk).start()

        @pl.when(step < 2)
        def _():
            window[:, :, pl.ds(pl.multiple_of(step * width, width), width)] = residual

        flat = residual.reshape(2 * rows, width)
        for block in range(2 * REACH + 1):
            outer[block] += lax.dot_general(
                flat,
                rows_of(block, chunk),
                (((1,), (1,)), ((), ())),
                preferred_element_type=jnp.float32,
            )

    def correlate():
        offset = lax.rem(me + shots - REACH, tiles) * rows
        real = jnp.zeros((rows, rows), jnp.float32)
        imag = jnp.zeros((rows, rows), jnp.float32)
        for block in range(2 * REACH + 1):
            spot = pl.ds(pl.multiple_of(offset + block * rows, rows), rows)
            resid_re = window[0, :, spot].astype(jnp.float32)
            resid_im = window[1, :, spot].astype(jnp.float32)
            resp_re = response(0, block)
            resp_im = response(1, block)
            real += resp_re * resid_re + resp_im * resid_im
            imag += resp_re * resid_im - resp_im * resid_re
        line = lax.broadcasted_iota(jnp.int32, waves.shape, 0)
        cosine = jnp.sum(jnp.where(line == freq, waves[...], 0.0), axis=0, keepdims=True)
        sine = jnp.sum(jnp.where(line == freq + freqs, waves[...], 0.0), axis=0, keepdims=True)
        series = jnp.sum(imag) * sine - jnp.sum(real) * cosine
        return jnp.broadcast_to(series, sums.shape[2:])

    def body(step, carry):
        @pl.when(step < chunks)
        def _():
            chunk = lax.rem(left_first + step, chunks)
            hop(0, chunk).wait_recv()
            hop(2, chunk).start()
            chunk = lax.rem(right_first + step, chunks)
            hop(1, chunk).wait_recv()
            hop(3, chunk).start()

        @pl.when(step < chunks - PRE)
        def _():
            chunk = lax.rem(own_first + step + PRE, chunks)
            load_own(chunk).wait()
            for stream in range(2):
                hop(stream, chunk).start()

        @pl.when(step >= LAG)
        def _():
            work(step - LAG)

        @pl.when(step == LAG + 1)
        def _():
            sum_send(0, correlate())

        for level in range(4):

            @pl.when(step == LAG + 3 + 2 * level)
            def _(level=level):
                total = sum_take(level)
                if level < 3:
                    sum_send(level + 1, total)
                else:
                    scale = 1.0 / math.sqrt(shots * rows * rows * (2 * REACH + 1))
                    wavelet_grad[...] = total * scale

        return carry

    lax.fori_loop(0, chunks + LAG, body, 0)

    for block in range(2 * REACH + 1):
        spot = pl.ds(block * rows, rows)
        low, high = pl.ds(0, rows), pl.ds(rows, rows)
        real = outer[block, low, low] + outer[block, high, high]
        imag = outer[block, high, low] - outer[block, low, high]
        grad[0, 0, :, spot] = real * inside(block)
        grad[0, 1, :, spot] = imag * inside(block)

    for slot in range(2):
        out_copy(slot, 0).wait()
    for level in range(4):
        for step in range(1, RADIX):
            exchange(level, step).wait_send()

    def drain(chunk, carry):
        for stream in range(4):
            hop(stream, chunk).wait_send()
        return carry

    lax.fori_loop(0, chunks, drain, 0)


def on_device(shots, freqs, data, primaries, wavelet, cover_ids, cover_counts):
    _, _, rows, width = data.shape
    chunks = width // RB
    band = primaries.shape[3]
    times = np.arange(NT, dtype=np.float32)
    phase = np.stack(
        [np.float32(2.0 * math.pi * (f + 1)) * times / np.float32(NT) for f in range(freqs)]
    )
    waves = jnp.asarray(np.concatenate([np.cos(phase), np.sin(phase)]).astype(np.float32))
    vmem = pl.BlockSpec(memory_space=pltpu.VMEM)
    hbm = pl.BlockSpec(memory_space=pl.ANY)
    blocks = 2 * REACH + 1
    dma = pltpu.SemaphoreType.DMA
    misfit, grad, series = pl.pallas_call(
        functools.partial(kernel, (shots, freqs, chunks, rows)),
        out_shape=(
            jax.ShapeDtypeStruct(data.shape, jnp.bfloat16),
            jax.ShapeDtypeStruct((1, 2, rows, band), jnp.float32),
            jax.ShapeDtypeStruct((8, NT), jnp.float32),
        ),
        in_specs=[hbm, vmem, pl.BlockSpec(memory_space=pltpu.SMEM), vmem, vmem, vmem],
        out_specs=(hbm, vmem, vmem),
        scratch_shapes=[
            pltpu.VMEM((2, rows, width), jnp.bfloat16),
            pltpu.VMEM((chunks, 2, rows, RB), jnp.bfloat16),
            pltpu.VMEM((4, chunks, 2, rows, RB), jnp.bfloat16),
            pltpu.VMEM((blocks, 2 * rows, 2 * rows), jnp.bfloat16),
            pltpu.VMEM((blocks, 2 * rows, 2 * rows), jnp.float32),
            pltpu.VMEM((2, 2, rows, RB), jnp.bfloat16),
            pltpu.VMEM((2, rows, 2 * RB), jnp.bfloat16),
            pltpu.VMEM((4, RADIX, 8, NT), jnp.float32),
            dma((chunks,)),
            dma((1,)),
            dma((2,)),
            dma((4, chunks)),
            dma((4, chunks)),
            dma((4, RADIX - 1)),
            dma((4, RADIX)),
        ],
        compiler_params=pltpu.CompilerParams(
            collective_id=0, has_side_effects=True, vmem_limit_bytes=48 * 1024 * 1024
        ),
    )(data, primaries, wavelet, cover_ids, cover_counts.reshape(rows, 1), waves)
    return misfit, grad, series[0]


def solution(mesh):
    in_specs = (
        P("freq", None, "shot", None),
        P("freq", None, "shot", None),
        P("freq", None),
        P("shot", None),
        P("shot"),
    )
    out_specs = (P("freq", None, "shot", None), P("freq", None, "shot", None), P())
    return jax.shard_map(
        functools.partial(on_device, mesh.shape["shot"], mesh.shape["freq"]),
        mesh=mesh,
        in_specs=in_specs,
        out_specs=out_specs,
        check_vma=False,
    )
```

time: 499 us -> 217 us (0.43)
  the two profiles are of different devices: /device:TPU:1 before, /device:TPU:10 now
where the time goes in v1:
time: 217 us
  Pallas kernels  209 us (96%)
  local copies, waits for them, and re-layouts  7.22 us (3%)
    pallas_call x1, Pallas kernels, on_device(): pl.pallas_call(functools.partial(kernel, (shots, freqs, chunks, rows)), o...  209 us
    unnamed x9, local copies, waits for them, and re-layouts  5.95 us

profile of v1, /device:TPU:10, one launch (start us, length us, event | category | flops | bytes accessed | tf_op | source)
XLA Modules:
  0.0 217.2 jit_solution(16117845871061477245)
XLA Ops:
  0.6 0.8 copy.9.ids
  1.4 0.8 copy.10.counts
  2.2 0.0 copy-start
  2.2 1.0 copy-done
  3.2 0.0 copy-start.1
  3.2 0.7 copy-done.1
  3.8 0.0 copy-start.2
  3.8 0.7 copy-done.2
  4.5 209.3 %shard_map.85 = (bf16[1,2,128,8192]{3,2,1,0:T(8,128)(2,1)S(1)}, f32[1,2,128,640]{3,2,1,0:T(8,128)S(1)}, f32[8,128]{1,0:T(8,128)S(1)}) custom-call(bf16[1,2,128,8192]{3,2,1,0:T(8,128)(2,1)} %data.1, bf16[1,2,128,640]{3,2,1,0:T(8,128)(2,1)S(1)} %copy-done, f32[1,2]{1,0:T(1,128)S(1)} %copy-done.2, s32[128,8]{1,0:T(8,128)S(1)} %copy.9.ids, ...), custom_call_target="tpu_custom_call" | custom-call | tf_op jit(solution)/shard_map/pallas_call | solution.py:319
  213.8 0.5 slice_bitcast_fusion
  214.3 2.0 copy.13
  216.3 0.8 copy.14
Async XLA Ops:
  2.2 1.0 copy-start
  3.2 0.7 copy-start.1
  3.8 0.7 copy-start.2

commit v2 on v1

--- a/solution.py
+++ b/solution.py
@@ -12,20 +12,22 @@
 RB = 512
 NT = 128
 REACH = 2
-PRE = 3
-LAG = 4
-RADIX = 4
+PRE = 6
+LAG = 5
+TAKE = 11
+RADIX = 16
+LEVELS = 2
 MESH = pl.DeviceIdType.MESH
 
 
 def kernel(
     dims,
     data,
-    prim,
-    wave,
-    ids,
-    counts,
-    waves,
+    prim_hbm,
+    wave_hbm,
+    ids_hbm,
+    counts_hbm,
+    waves_hbm,
     misfit,
     grad,
     wavelet_grad,
@@ -37,6 +39,13 @@
     stage,
     window,
     sums,
+    prim,
+    wave,
+    ids,
+    counts,
+    waves,
+    cover,
+    small_sem,
     own_sem,
     rec_sem,
     out_sem,
@@ -81,13 +90,17 @@
             device_id_type=MESH,
         )
 
-    digits = [freq, lax.rem(me, 4), lax.rem(lax.div(me, 4), 4), lax.div(me, 16)]
+    line = RADIX // 2
+    digits = [
+        lax.rem(freq, 2) * line + lax.rem(me, line),
+        lax.div(freq, 2) * line + lax.div(me, line),
+    ]
 
     def partner(level, digit):
+        first, second = lax.rem(digit, line), lax.div(digit, line)
         if level == 0:
-            return (me, digit)
-        scale = (1, 4, 16)[level - 1]
-        return (me + (digit - digits[level]) * scale, freq)
+            return (me - lax.rem(me, line) + first, freq - lax.rem(freq, 2) + second)
+        return (first * line + lax.rem(me, line), second * 2 + lax.rem(freq, 2))
 
     def exchange(level, step):
         digit = lax.rem(digits[level] + step, RADIX)
@@ -126,12 +139,26 @@
 
     for step in range(chunks):
         load_own(lax.rem(own_first + step, chunks)).start()
+    small = [
+        pltpu.make_async_copy(source, target, small_sem.at[spot])
+        for spot, (source, target) in enumerate(
+            [
+                (wave_hbm, wave),
+                (prim_hbm, prim),
+                (ids_hbm, ids),
+                (counts_hbm, counts),
+                (waves_hbm, waves),
+            ]
+        )
+    ]
+    for copy in small:
+        copy.start()
     load_rec.start()
 
     barrier = pltpu.get_barrier_semaphore()
     for target in (left, right):
         pl.semaphore_signal(barrier, inc=1, device_id=(target, freq), device_id_type=MESH)
-    for level in range(4):
+    for level in range(LEVELS):
         for step in range(1, RADIX):
             pl.semaphore_signal(
                 barrier,
@@ -139,8 +166,9 @@
                 device_id=partner(level, lax.rem(digits[level] + step, RADIX)),
                 device_id_type=MESH,
             )
-    pl.semaphore_wait(barrier, 2 + 4 * (RADIX - 1))
-
+    pl.semaphore_wait(barrier, 2 + LEVELS * (RADIX - 1))
+
+    small[0].wait()
     diagonal = lax.broadcasted_iota(jnp.int32, (rows, rows), 0) == lax.broadcasted_iota(
         jnp.int32, (rows, rows), 1
     )
@@ -151,10 +179,20 @@
             spot = pl.ds(pl.multiple_of(lax.rem(me, tiles) * rows, rows), rows)
             for part in range(2):
                 tile = own[chunk, part, :, spot]
-                moved = (tile.astype(jnp.float32) - wave[0, part]).astype(jnp.bfloat16)
+                moved = (tile.astype(jnp.float32) - wave[pl.ds(0, 1), pl.ds(part, 1)]).astype(jnp.bfloat16)
                 own[chunk, part, :, spot] = jnp.where(diagonal, moved, tile)
         for stream in range(2):
             hop(stream, chunk).start()
+
+    for copy in small[1:]:
+        copy.wait()
+    entry = lax.broadcasted_iota(jnp.int32, ids.shape, 0)
+    listed = entry < counts[...]
+    cover[...] = jnp.zeros_like(cover)
+    for chunk in range(chunks):
+        hit = jnp.logical_and(ids[...] == chunk, listed)
+        cover[pl.ds(chunk, 1), :] = jnp.sum(jnp.where(hit, 1.0, 0.0), axis=0, keepdims=True)
+    cover[...] = cover[...].T
 
     def inside(block):
         there = me + block - REACH
@@ -195,9 +233,8 @@
             predicted += jnp.dot(
                 mix[block], rows_of(block, chunk), preferred_element_type=jnp.float32
             )
-        entry = lax.broadcasted_iota(jnp.int32, ids.shape, 1)
-        hit = jnp.logical_and(ids[...] == chunk, entry < counts[...])
-        mask = jnp.sum(jnp.where(hit, 1.0, 0.0), axis=1, keepdims=True)
+        lane = lax.broadcasted_iota(jnp.int32, cover.shape, 1)
+        mask = jnp.sum(jnp.where(lane == chunk, cover[...], 0.0), axis=1, keepdims=True)
         record = rec[:, :, columns].astype(jnp.float32)
         residual = (mask[None] * (record + predicted.reshape(2, rows, width))).astype(
             jnp.bfloat16
@@ -266,16 +303,9 @@
         def _():
             sum_send(0, correlate())
 
-        for level in range(4):
-
-            @pl.when(step == LAG + 3 + 2 * level)
-            def _(level=level):
-                total = sum_take(level)
-                if level < 3:
-                    sum_send(level + 1, total)
-                else:
-                    scale = 1.0 / math.sqrt(shots * rows * rows * (2 * REACH + 1))
-                    wavelet_grad[...] = total * scale
+        @pl.when(step == TAKE)
+        def _():
+            sum_send(1, sum_take(0))
 
         return carry
 
@@ -289,9 +319,12 @@
         grad[0, 0, :, spot] = real * inside(block)
         grad[0, 1, :, spot] = imag * inside(block)
 
+    scale = 1.0 / math.sqrt(shots * rows * rows * (2 * REACH + 1))
+    wavelet_grad[...] = sum_take(1) * scale
+
     for slot in range(2):
         out_copy(slot, 0).wait()
-    for level in range(4):
+    for level in range(LEVELS):
         for step in range(1, RADIX):
             exchange(level, step).wait_send()
 
@@ -313,7 +346,7 @@
     )
     waves = jnp.asarray(np.concatenate([np.cos(phase), np.sin(phase)]).astype(np.float32))
     vmem = pl.BlockSpec(memory_space=pltpu.VMEM)
-    hbm = pl.BlockSpec(memory_space=pl.ANY)
+    hbm = pl.BlockSpec(memory_space=pltpu.HBM)
     blocks = 2 * REACH + 1
     dma = pltpu.SemaphoreType.DMA
     misfit, grad, series = pl.pallas_call(
@@ -321,10 +354,10 @@
         out_shape=(
             jax.ShapeDtypeStruct(data.shape, jnp.bfloat16),
             jax.ShapeDtypeStruct((1, 2, rows, band), jnp.float32),
-            jax.ShapeDtypeStruct((8, NT), jnp.float32),
+            jax.ShapeDtypeStruct((1, NT), jnp.float32),
         ),
-        in_specs=[hbm, vmem, pl.BlockSpec(memory_space=pltpu.SMEM), vmem, vmem, vmem],
-        out_specs=(hbm, vmem, vmem),
+        in_specs=[hbm] * 6,
+        out_specs=(pl.BlockSpec(memory_space=pl.ANY), vmem, vmem),
         scratch_shapes=[
             pltpu.VMEM((2, rows, width), jnp.bfloat16),
             pltpu.VMEM((chunks, 2, rows, RB), jnp.bfloat16),
@@ -333,19 +366,38 @@
             pltpu.VMEM((blocks, 2 * rows, 2 * rows), jnp.float32),
             pltpu.VMEM((2, 2, rows, RB), jnp.bfloat16),
             pltpu.VMEM((2, rows, 2 * RB), jnp.bfloat16),
-            pltpu.VMEM((4, RADIX, 8, NT), jnp.float32),
+            pltpu.VMEM((LEVELS, RADIX, 1, NT), jnp.float32),
+            pltpu.VMEM(primaries.shape, jnp.bfloat16),
+            pltpu.VMEM(wavelet.shape, jnp.float32),
+            pltpu.VMEM(cover_ids.shape[::-1], jnp.int32),
+            pltpu.VMEM((1, rows), jnp.int32),
+            pltpu.VMEM(waves.shape, jnp.float32),
+            pltpu.VMEM((rows, rows), jnp.float32),
+            dma((5,)),
             dma((chunks,)),
             dma((1,)),
             dma((2,)),
             dma((4, chunks)),
             dma((4, chunks)),
-            dma((4, RADIX - 1)),
-            dma((4, RADIX)),
+            dma((LEVELS, RADIX - 1)),
+            dma((LEVELS, RADIX)),
         ],
         compiler_params=pltpu.CompilerParams(
             collective_id=0, has_side_effects=True, vmem_limit_bytes=48 * 1024 * 1024
         ),
-    )(data, primaries, wavelet, cover_ids, cover_counts.reshape(rows, 1), waves)
+    )(
+        *(
+            pltpu.with_memory_space_constraint(operand, pltpu.HBM)
+            for operand in (
+                data,
+                primaries,
+                wavelet,
+                cover_ids.T,
+                cover_counts.reshape(1, rows),
+                waves,
+            )
+        )
+    )
     return misfit, grad, series[0]
 
 

time: 217 us -> 202 us (0.931)
  the two profiles are of different devices: /device:TPU:10 before, /device:TPU:1 now
where the time goes in v2:
time: 202 us
  Pallas kernels  198 us (98%)
  local copies, waits for them, and re-layouts  3.36 us (2%)
    pallas_call x1, Pallas kernels, on_device(): pl.pallas_call(functools.partial(kernel, (shots, freqs, chunks, rows)), o...  198 us

profile of v2, /device:TPU:1, one launch (start us, length us, event | category | flops | bytes accessed | tf_op | source)
XLA Modules:
  0.0 202.0 jit_solution(18082644790006033601)
XLA Ops:
  0.6 198.0 %shard_map.85 = (bf16[1,2,128,8192]{3,2,1,0:T(8,128)(2,1)S(1)}, f32[1,2,128,640]{3,2,1,0:T(8,128)S(1)}, f32[1,128]{1,0:T(1,128)S(1)}) custom-call(bf16[1,2,128,8192]{3,2,1,0:T(8,128)(2,1)} %data.1, bf16[1,2,128,640]{3,2,1,0:T(8,128)(2,1)} %prim_hbm.1, f32[1,2]{1,0:T(1,128)} %wave_hbm.1, s32[8,128]{1,0:T(8,128)} %bitcast.4, s32[1,128]{1,0:T(1,128)} %bitcast.5, ...), custom_call_target="tpu_custom_call" | custom-call | tf_op jit(solution)/shard_map/pallas_call | solution.py:352
  198.7 2.0 copy.12
  200.7 0.8 copy.13
  201.5 0.5 copy.14

commit v3 on v2

--- a/solution.py
+++ b/solution.py
@@ -14,6 +14,7 @@
 REACH = 2
 PRE = 6
 LAG = 5
+BEHIND = 2
 TAKE = 11
 RADIX = 16
 LEVELS = 2
@@ -36,7 +37,6 @@
     near,
     mix,
     outer,
-    stage,
     window,
     sums,
     prim,
@@ -48,7 +48,6 @@
     small_sem,
     own_sem,
     rec_sem,
-    out_sem,
     send_sem,
     recv_sem,
     sum_send_sem,
@@ -62,13 +61,18 @@
     right = lax.rem(me + 1, shots)
     left = lax.rem(me + shots - 1, shots)
 
-    def first_of(block):
-        return lax.rem(lax.div(block, tiles) + chunks - 1, chunks)
-
-    own_first = first_of(me)
-    left_first = first_of(left)
-    right_first = first_of(right)
-    work_first = lax.rem(lax.div(me + shots - REACH, tiles), chunks)
+    def turn(first, count, step):
+        later = step - count
+        past = jnp.where(later < first, later, later + count)
+        past = jnp.where(first + count > chunks, later + first + count - chunks, past)
+        return jnp.where(step < count, lax.rem(first + step, chunks), past)
+
+    def sent(block, step):
+        first = lax.rem(lax.div(block, tiles) + chunks - 1, chunks)
+        return turn(first, 3, step)
+
+    def worked(step):
+        return turn(lax.rem(lax.div(me + shots - REACH, tiles), chunks), 2, step)
 
     def load_own(chunk):
         columns = pl.ds(pl.multiple_of(chunk * width, width), width)
@@ -77,6 +81,10 @@
         )
 
     load_rec = pltpu.make_async_copy(data.at[0], rec, rec_sem.at[0])
+
+    inner = jnp.logical_and(me > 0, me < shots - 1)
+    sends = (me < shots - 1, me > 0, inner, inner)
+    takes = (me > 0, me < shots - 1, me > 1, me < shots - 2)
 
     def hop(stream, chunk):
         src = own.at[chunk] if stream < 2 else near.at[stream - 2, chunk]
@@ -138,7 +146,7 @@
         return total
 
     for step in range(chunks):
-        load_own(lax.rem(own_first + step, chunks)).start()
+        load_own(sent(me, step)).start()
     small = [
         pltpu.make_async_copy(source, target, small_sem.at[spot])
         for spot, (source, target) in enumerate(
@@ -156,8 +164,12 @@
     load_rec.start()
 
     barrier = pltpu.get_barrier_semaphore()
-    for target in (left, right):
-        pl.semaphore_signal(barrier, inc=1, device_id=(target, freq), device_id_type=MESH)
+    for target, there in ((left, sends[1]), (right, sends[0])):
+
+        @pl.when(there)
+        def _(target=target):
+            pl.semaphore_signal(barrier, inc=1, device_id=(target, freq), device_id_type=MESH)
+
     for level in range(LEVELS):
         for step in range(1, RADIX):
             pl.semaphore_signal(
@@ -166,14 +178,14 @@
                 device_id=partner(level, lax.rem(digits[level] + step, RADIX)),
                 device_id_type=MESH,
             )
-    pl.semaphore_wait(barrier, 2 + LEVELS * (RADIX - 1))
+    pl.semaphore_wait(barrier, jnp.where(inner, 2, 1) + LEVELS * (RADIX - 1))
 
     small[0].wait()
     diagonal = lax.broadcasted_iota(jnp.int32, (rows, rows), 0) == lax.broadcasted_iota(
         jnp.int32, (rows, rows), 1
     )
     for step in range(PRE):
-        chunk = lax.rem(own_first + step, chunks)
+        chunk = sent(me, step)
         load_own(chunk).wait()
         if step == 1:
             spot = pl.ds(pl.multiple_of(lax.rem(me, tiles) * rows, rows), rows)
@@ -182,7 +194,7 @@
                 moved = (tile.astype(jnp.float32) - wave[pl.ds(0, 1), pl.ds(part, 1)]).astype(jnp.bfloat16)
                 own[chunk, part, :, spot] = jnp.where(diagonal, moved, tile)
         for stream in range(2):
-            hop(stream, chunk).start()
+            pl.when(sends[stream])(hop(stream, chunk).start)
 
     for copy in small[1:]:
         copy.wait()
@@ -210,23 +222,26 @@
         mix[block, pl.ds(rows, rows), pl.ds(0, rows)] = imag.astype(jnp.bfloat16)
         mix[block, pl.ds(rows, rows), pl.ds(rows, rows)] = real.astype(jnp.bfloat16)
     outer[...] = jnp.zeros_like(outer)
+    for stream in range(4):
+
+        @pl.when(jnp.logical_not(takes[stream]))
+        def _(stream=stream):
+            def clear(chunk, carry):
+                near[stream, chunk] = jnp.zeros(near.shape[2:], near.dtype)
+                return carry
+
+            lax.fori_loop(0, chunks, clear, 0)
+
     load_rec.wait()
 
     def rows_of(block, chunk):
         ref = own.at[chunk] if block == REACH else near.at[(2, 0, -1, 1, 3)[block], chunk]
         return ref[...].reshape(2 * rows, width)
 
-    def out_copy(slot, chunk):
-        columns = pl.ds(pl.multiple_of(chunk * width, width), width)
-        return pltpu.make_async_copy(
-            stage.at[slot], misfit.at[0, :, :, columns], out_sem.at[slot]
-        )
-
     def work(step):
-        chunk = lax.rem(work_first + step, chunks)
-        slot = lax.rem(step, 2)
+        chunk = worked(step)
         for stream in (2, 3):
-            hop(stream, chunk).wait_recv()
+            pl.when(takes[stream])(hop(stream, chunk).wait_recv)
         columns = pl.ds(pl.multiple_of(chunk * width, width), width)
         predicted = jnp.dot(mix[0], rows_of(0, chunk), preferred_element_type=jnp.float32)
         for block in range(1, 2 * REACH + 1):
@@ -240,12 +255,7 @@
             jnp.bfloat16
         )
 
-        @pl.when(step >= 2)
-        def _():
-            out_copy(slot, chunk).wait()
-
-        stage[slot] = residual
-        out_copy(slot, chunk).start()
+        misfit[0, :, :, columns] = residual
 
         @pl.when(step < 2)
         def _():
@@ -281,23 +291,32 @@
     def body(step, carry):
         @pl.when(step < chunks)
         def _():
-            chunk = lax.rem(left_first + step, chunks)
-            hop(0, chunk).wait_recv()
-            hop(2, chunk).start()
-            chunk = lax.rem(right_first + step, chunks)
-            hop(1, chunk).wait_recv()
-            hop(3, chunk).start()
+            chunk = sent(left, step)
+            pl.when(takes[0])(hop(0, chunk).wait_recv)
+            pl.when(sends[2])(hop(2, chunk).start)
+            chunk = sent(right, step)
+            pl.when(takes[1])(hop(1, chunk).wait_recv)
+            pl.when(sends[3])(hop(3, chunk).start)
 
         @pl.when(step < chunks - PRE)
         def _():
-            chunk = lax.rem(own_first + step + PRE, chunks)
+            chunk = sent(me, step + PRE)
             load_own(chunk).wait()
             for stream in range(2):
-                hop(stream, chunk).start()
+                pl.when(sends[stream])(hop(stream, chunk).start)
 
         @pl.when(step >= LAG)
         def _():
             work(step - LAG)
+            chunk = sent(me, step - LAG)
+            for stream in range(2):
+                pl.when(sends[stream])(hop(stream, chunk).wait_send)
+
+        @pl.when(step >= LAG + BEHIND)
+        def _():
+            past = step - LAG - BEHIND
+            pl.when(sends[2])(hop(2, sent(left, past)).wait_send)
+            pl.when(sends[3])(hop(3, sent(right, past)).wait_send)
 
         @pl.when(step == LAG + 1)
         def _():
@@ -306,6 +325,14 @@
         @pl.when(step == TAKE)
         def _():
             sum_send(1, sum_take(0))
+
+        @pl.when(step == chunks + LAG - 3)
+        def _():
+            scale = 1.0 / math.sqrt(shots * rows * rows * (2 * REACH + 1))
+            wavelet_grad[...] = sum_take(1) * scale
+            for level in range(LEVELS):
+                for near_by in range(1, RADIX):
+                    exchange(level, near_by).wait_send()
 
         return carry
 
@@ -319,21 +346,25 @@
         grad[0, 0, :, spot] = real * inside(block)
         grad[0, 1, :, spot] = imag * inside(block)
 
-    scale = 1.0 / math.sqrt(shots * rows * rows * (2 * REACH + 1))
-    wavelet_grad[...] = sum_take(1) * scale
-
-    for slot in range(2):
-        out_copy(slot, 0).wait()
-    for level in range(LEVELS):
-        for step in range(1, RADIX):
-            exchange(level, step).wait_send()
-
-    def drain(chunk, carry):
-        for stream in range(4):
-            hop(stream, chunk).wait_send()
-        return carry
-
-    lax.fori_loop(0, chunks, drain, 0)
+    for past in range(chunks - BEHIND, chunks):
+        pl.when(sends[2])(hop(2, sent(left, past)).wait_send)
+        pl.when(sends[3])(hop(3, sent(right, past)).wait_send)
+
+
+def flush(misfit, grad, series, misfit_out, grad_out, series_out, sems):
+    parts = [(series, series_out), (grad, grad_out)]
+    for part in range(2):
+        for spot in range(8):
+            rows = pl.ds(spot * 16, 16)
+            parts.append((misfit.at[0, part, rows], misfit_out.at[0, part, rows]))
+    copies = [
+        pltpu.make_async_copy(source, target, sems.at[spot])
+        for spot, (source, target) in enumerate(parts)
+    ]
+    for copy in copies:
+        copy.start()
+    for copy in copies:
+        copy.wait()
 
 
 def on_device(shots, freqs, data, primaries, wavelet, cover_ids, cover_counts):
@@ -357,14 +388,13 @@
             jax.ShapeDtypeStruct((1, NT), jnp.float32),
         ),
         in_specs=[hbm] * 6,
-        out_specs=(pl.BlockSpec(memory_space=pl.ANY), vmem, vmem),
+        out_specs=(vmem, vmem, vmem),
         scratch_shapes=[
             pltpu.VMEM((2, rows, width), jnp.bfloat16),
             pltpu.VMEM((chunks, 2, rows, RB), jnp.bfloat16),
             pltpu.VMEM((4, chunks, 2, rows, RB), jnp.bfloat16),
             pltpu.VMEM((blocks, 2 * rows, 2 * rows), jnp.bfloat16),
             pltpu.VMEM((blocks, 2 * rows, 2 * rows), jnp.float32),
-            pltpu.VMEM((2, 2, rows, RB), jnp.bfloat16),
             pltpu.VMEM((2, rows, 2 * RB), jnp.bfloat16),
             pltpu.VMEM((LEVELS, RADIX, 1, NT), jnp.float32),
             pltpu.VMEM(primaries.shape, jnp.bfloat16),
@@ -376,7 +406,6 @@
             dma((5,)),
             dma((chunks,)),
             dma((1,)),
-            dma((2,)),
             dma((4, chunks)),
             dma((4, chunks)),
             dma((LEVELS, RADIX - 1)),
@@ -398,6 +427,15 @@
             )
         )
     )
+    results = (misfit, grad, series)
+    misfit, grad, series = pl.pallas_call(
+        flush,
+        out_shape=tuple(pltpu.HBM(part.shape, part.dtype) for part in results),
+        in_specs=[vmem] * 3,
+        out_specs=(hbm,) * 3,
+        scratch_shapes=[dma((18,))],
+        compiler_params=pltpu.CompilerParams(vmem_limit_bytes=8 * 1024 * 1024),
+    )(*(pltpu.with_memory_space_constraint(part, pltpu.VMEM) for part in results))
     return misfit, grad, series[0]
 
 

time: 202 us -> 199 us (0.985); the launches traced: 202 us -> 196 us
  local copies, waits for them, and re-layouts: 3.36 us -> 0 us
  Pallas kernels: 198 us -> 195 us
    pallas_call x1, Pallas kernels: 198 us -> 193 us  [on_device(): pl.pallas_call(functools.partial(kernel, (shots, freqs, chunks, rows)), o...]
    unnamed x3 -> x0, local copies, waits for them, and re-layouts: 3.36 us -> none
    pallas_call x0 -> x1, Pallas kernels: none -> 2.36 us  [on_device(): pl.pallas_call(flush, out_shape=tuple((pltpu.HBM(part.shape, part.dtype)...]
where the time goes in v3:
time: 199 us; the launch traced here: 196 us
  Pallas kernels  195 us (98%)
    pallas_call x1, Pallas kernels, on_device(): pl.pallas_call(functools.partial(kernel, (shots, freqs, chunks, rows)), o...  193 us

profile of v3, /device:TPU:1, one launch (start us, length us, event | category | flops | bytes accessed | tf_op | source)
XLA Modules:
  0.0 196.1 jit_solution(5695938309135688103)
XLA Ops:
  0.6 193.1 %shard_map.85 = (bf16[1,2,128,8192]{3,2,1,0:T(8,128)(2,1)S(1)}, f32[1,2,128,640]{3,2,1,0:T(8,128)S(1)}, f32[1,128]{1,0:T(1,128)S(1)}) custom-call(bf16[1,2,128,8192]{3,2,1,0:T(8,128)(2,1)} %data.1, bf16[1,2,128,640]{3,2,1,0:T(8,128)(2,1)} %prim_hbm.1, f32[1,2]{1,0:T(1,128)} %wave_hbm.1, s32[8,128]{1,0:T(8,128)} %bitcast.3, s32[1,128]{1,0:T(1,128)} %bitcast.4, ...), custom_call_target="tpu_custom_call" | custom-call | tf_op jit(solution)/shard_map/pallas_call | solution.py:383
  193.7 2.4 %shard_map.86 = (bf16[1,2,128,8192]{3,2,1,0:T(8,128)(2,1)}, f32[1,2,128,640]{3,2,1,0:T(8,128)}, f32[1,128]{1,0:T(1,128)}) custom-call(bf16[1,2,128,8192]{3,2,1,0:T(8,128)(2,1)S(1)} %get-tuple-element.9.misfit, f32[1,2,128,640]{3,2,1,0:T(8,128)S(1)} %get-tuple-element.10.grad, f32[1,128]{1,0:T(1,128)S(1)} %get-tuple-element.11.series), custom_call_target="tpu_custom_call" | custom-call | tf_op jit(solution)/shard_map/pallas_call | solution.py:431

commit v4 on v3

--- a/solution.py
+++ b/solution.py
@@ -33,7 +33,6 @@
     grad,
     wavelet_grad,
     rec,
-    own,
     near,
     mix,
     outer,
@@ -54,7 +53,9 @@
     sum_recv_sem,
 ):
     shots, freqs, chunks, rows = dims
-    width = own.shape[3]
+    width = near.shape[4]
+    place = (1, 3, 0, 4)
+    band = 2 * REACH + 1
     tiles = width // rows
     me = lax.axis_index("shot")
     freq = lax.axis_index("freq")
@@ -77,7 +78,7 @@
     def load_own(chunk):
         columns = pl.ds(pl.multiple_of(chunk * width, width), width)
         return pltpu.make_async_copy(
-            data.at[0, :, :, columns], own.at[chunk], own_sem.at[chunk]
+            data.at[0, :, :, columns], near.at[chunk, REACH], own_sem.at[chunk]
         )
 
     load_rec = pltpu.make_async_copy(data.at[0], rec, rec_sem.at[0])
@@ -87,11 +88,11 @@
     takes = (me > 0, me < shots - 1, me > 1, me < shots - 2)
 
     def hop(stream, chunk):
-        src = own.at[chunk] if stream < 2 else near.at[stream - 2, chunk]
+        src = near.at[chunk, REACH if stream < 2 else place[stream - 2]]
         target = right if stream % 2 == 0 else left
         return pltpu.make_async_remote_copy(
             src_ref=src,
-            dst_ref=near.at[stream, chunk],
+            dst_ref=near.at[chunk, place[stream]],
             send_sem=send_sem.at[stream, chunk],
             recv_sem=recv_sem.at[stream, chunk],
             device_id=(target, freq),
@@ -145,8 +146,6 @@
             total = total + sums[level, digit]
         return total
 
-    for step in range(chunks):
-        load_own(sent(me, step)).start()
     small = [
         pltpu.make_async_copy(source, target, small_sem.at[spot])
         for spot, (source, target) in enumerate(
@@ -159,9 +158,11 @@
             ]
         )
     ]
-    for copy in small:
+    small[0].start()
+    for step in range(PRE):
+        load_own(sent(me, step)).start()
+    for copy in small[1:]:
         copy.start()
-    load_rec.start()
 
     barrier = pltpu.get_barrier_semaphore()
     for target, there in ((left, sends[1]), (right, sends[0])):
@@ -180,7 +181,6 @@
             )
     pl.semaphore_wait(barrier, jnp.where(inner, 2, 1) + LEVELS * (RADIX - 1))
 
-    small[0].wait()
     diagonal = lax.broadcasted_iota(jnp.int32, (rows, rows), 0) == lax.broadcasted_iota(
         jnp.int32, (rows, rows), 1
     )
@@ -188,14 +188,18 @@
         chunk = sent(me, step)
         load_own(chunk).wait()
         if step == 1:
+            small[0].wait()
             spot = pl.ds(pl.multiple_of(lax.rem(me, tiles) * rows, rows), rows)
             for part in range(2):
-                tile = own[chunk, part, :, spot]
+                tile = near[chunk, REACH, part, :, spot]
                 moved = (tile.astype(jnp.float32) - wave[pl.ds(0, 1), pl.ds(part, 1)]).astype(jnp.bfloat16)
-                own[chunk, part, :, spot] = jnp.where(diagonal, moved, tile)
+                near[chunk, REACH, part, :, spot] = jnp.where(diagonal, moved, tile)
         for stream in range(2):
             pl.when(sends[stream])(hop(stream, chunk).start)
 
+    for step in range(PRE, chunks):
+        load_own(sent(me, step)).start()
+    load_rec.start()
     for copy in small[1:]:
         copy.wait()
     entry = lax.broadcasted_iota(jnp.int32, ids.shape, 0)
@@ -217,37 +221,32 @@
     for block in range(2 * REACH + 1):
         real = response(0, block)
         imag = response(1, block)
-        mix[block, pl.ds(0, rows), pl.ds(0, rows)] = real.astype(jnp.bfloat16)
-        mix[block, pl.ds(0, rows), pl.ds(rows, rows)] = (-imag).astype(jnp.bfloat16)
-        mix[block, pl.ds(rows, rows), pl.ds(0, rows)] = imag.astype(jnp.bfloat16)
-        mix[block, pl.ds(rows, rows), pl.ds(rows, rows)] = real.astype(jnp.bfloat16)
+        upper, lower = pl.ds(0, rows), pl.ds(rows, rows)
+        first, second = pl.ds(2 * block * rows, rows), pl.ds((2 * block + 1) * rows, rows)
+        mix[upper, first] = real.astype(jnp.bfloat16)
+        mix[upper, second] = (-imag).astype(jnp.bfloat16)
+        mix[lower, first] = imag.astype(jnp.bfloat16)
+        mix[lower, second] = real.astype(jnp.bfloat16)
     outer[...] = jnp.zeros_like(outer)
     for stream in range(4):
 
         @pl.when(jnp.logical_not(takes[stream]))
         def _(stream=stream):
             def clear(chunk, carry):
-                near[stream, chunk] = jnp.zeros(near.shape[2:], near.dtype)
+                near[chunk, place[stream]] = jnp.zeros(near.shape[2:], near.dtype)
                 return carry
 
             lax.fori_loop(0, chunks, clear, 0)
 
     load_rec.wait()
-
-    def rows_of(block, chunk):
-        ref = own.at[chunk] if block == REACH else near.at[(2, 0, -1, 1, 3)[block], chunk]
-        return ref[...].reshape(2 * rows, width)
 
     def work(step):
         chunk = worked(step)
         for stream in (2, 3):
             pl.when(takes[stream])(hop(stream, chunk).wait_recv)
         columns = pl.ds(pl.multiple_of(chunk * width, width), width)
-        predicted = jnp.dot(mix[0], rows_of(0, chunk), preferred_element_type=jnp.float32)
-        for block in range(1, 2 * REACH + 1):
-            predicted += jnp.dot(
-                mix[block], rows_of(block, chunk), preferred_element_type=jnp.float32
-            )
+        nearby = near[chunk].reshape(2 * band * rows, width)
+        predicted = jnp.dot(mix[...], nearby, preferred_element_type=jnp.float32)
         lane = lax.broadcasted_iota(jnp.int32, cover.shape, 1)
         mask = jnp.sum(jnp.where(lane == chunk, cover[...], 0.0), axis=1, keepdims=True)
         record = rec[:, :, columns].astype(jnp.float32)
@@ -261,14 +260,12 @@
         def _():
             window[:, :, pl.ds(pl.multiple_of(step * width, width), width)] = residual
 
-        flat = residual.reshape(2 * rows, width)
-        for block in range(2 * REACH + 1):
-            outer[block] += lax.dot_general(
-                flat,
-                rows_of(block, chunk),
-                (((1,), (1,)), ((), ())),
-                preferred_element_type=jnp.float32,
-            )
+        outer[...] += lax.dot_general(
+            residual.reshape(2 * rows, width),
+            nearby,
+            (((1,), (1,)), ((), ())),
+            preferred_element_type=jnp.float32,
+        )
 
     def correlate():
         offset = lax.rem(me + shots - REACH, tiles) * rows
@@ -340,9 +337,10 @@
 
     for block in range(2 * REACH + 1):
         spot = pl.ds(block * rows, rows)
-        low, high = pl.ds(0, rows), pl.ds(rows, rows)
-        real = outer[block, low, low] + outer[block, high, high]
-        imag = outer[block, high, low] - outer[block, low, high]
+        upper, lower = pl.ds(0, rows), pl.ds(rows, rows)
+        first, second = pl.ds(2 * block * rows, rows), pl.ds((2 * block + 1) * rows, rows)
+        real = outer[upper, first] + outer[lower, second]
+        imag = outer[lower, first] - outer[upper, second]
         grad[0, 0, :, spot] = real * inside(block)
         grad[0, 1, :, spot] = imag * inside(block)
 
@@ -391,10 +389,9 @@
         out_specs=(vmem, vmem, vmem),
         scratch_shapes=[
             pltpu.VMEM((2, rows, width), jnp.bfloat16),
-            pltpu.VMEM((chunks, 2, rows, RB), jnp.bfloat16),
-            pltpu.VMEM((4, chunks, 2, rows, RB), jnp.bfloat16),
-            pltpu.VMEM((blocks, 2 * rows, 2 * rows), jnp.bfloat16),
-            pltpu.VMEM((blocks, 2 * rows, 2 * rows), jnp.float32),
+            pltpu.VMEM((chunks, blocks, 2, rows, RB), jnp.bfloat16),
+            pltpu.VMEM((2 * rows, 2 * band), jnp.bfloat16),
+            pltpu.VMEM((2 * rows, 2 * band), jnp.float32),
             pltpu.VMEM((2, rows, 2 * RB), jnp.bfloat16),
             pltpu.VMEM((LEVELS, RADIX, 1, NT), jnp.float32),
             pltpu.VMEM(primaries.shape, jnp.bfloat16),

time: 199 us -> 199 us (level)
  no operation moved by 1% of the time
where the time goes in v4:
time: 199 us; the launch traced here: 196 us
  Pallas kernels  195 us (98%)
    pallas_call x1, Pallas kernels, on_device(): pl.pallas_call(functools.partial(kernel, (shots, freqs, chunks, rows)), o...  193 us

profile of v4, /device:TPU:1, one launch (start us, length us, event | category | flops | bytes accessed | tf_op | source)
XLA Modules:
  0.0 196.0 jit_solution(13604615920046875450)
XLA Ops:
  0.6 193.0 %shard_map.85 = (bf16[1,2,128,8192]{3,2,1,0:T(8,128)(2,1)S(1)}, f32[1,2,128,640]{3,2,1,0:T(8,128)S(1)}, f32[1,128]{1,0:T(1,128)S(1)}) custom-call(bf16[1,2,128,8192]{3,2,1,0:T(8,128)(2,1)} %data.1, bf16[1,2,128,640]{3,2,1,0:T(8,128)(2,1)} %prim_hbm.1, f32[1,2]{1,0:T(1,128)} %wave_hbm.1, s32[8,128]{1,0:T(8,128)} %bitcast.3, s32[1,128]{1,0:T(1,128)} %bitcast.4, ...), custom_call_target="tpu_custom_call" | custom-call | tf_op jit(solution)/shard_map/pallas_call | solution.py:381
  193.7 2.4 %shard_map.86 = (bf16[1,2,128,8192]{3,2,1,0:T(8,128)(2,1)}, f32[1,2,128,640]{3,2,1,0:T(8,128)}, f32[1,128]{1,0:T(1,128)}) custom-call(bf16[1,2,128,8192]{3,2,1,0:T(8,128)(2,1)S(1)} %get-tuple-element.9.misfit, f32[1,2,128,640]{3,2,1,0:T(8,128)S(1)} %get-tuple-element.10.grad, f32[1,128]{1,0:T(1,128)S(1)} %get-tuple-element.11.series), custom_call_target="tpu_custom_call" | custom-call | tf_op jit(solution)/shard_map/pallas_call | solution.py:428
